TPU v7x, 32 devices: a whole 2x2x4 slice. The times are simulated.
32 devices in a mesh: row: 4 (over y, x), col: 8 (over z, core).
Axes of the slice: x: 2, y: 2, z: 4, core: 2. Of those that a mesh axis runs over, the one named last changes fastest.
Arguments:
- anc_inverse: float32 [10240, 10240], P('row', 'col'), may hold values from -0.0625 to 0.0625
- lower_anc: float32 [10240, 3, 384], P('col', None, 'row'), may hold values from -1.5 to 1.5
- upper_anc: float32 [10240, 3, 384], P('row', None, 'col'), may hold values from -0.75 to 0.75
- lower_edge: float32 [2, 384, 384], replicated, may hold values from -0.3125 to 0.3125
- upper_edge: float32 [2, 384, 384], replicated, may hold values from -0.3125 to 0.3125
- diag_inverse: float32 [3, 384, 384], replicated, may hold values from -6 to 6
- tile_mask: int32 [3, 80, 3], replicated, may hold values 0 or 1
Outputs:
- x_blocks: float32 [10240, 3, 384], P(('row', 'col'))
- y_blocks: float32 [8, 4, 320, 3, 384], P('col', 'row')
- z_blocks: float32 [3, 384, 384], P(None, 'row', 'col')
- cross_blocks: float32 [2, 2, 384, 384], P(None, None, 'row', 'col')
All inputs are finite; a program needn't handle non-finite values.
Results may differ from a plain program's by a relative error of at most 0.0001.
Values sent between devices are 32-bit elements; how exact they have to be, the bound alone decides.
A program may use at most 128 MiB of HBM per device.

v0:
```python
import jax
import jax.numpy as jnp
from jax import lax
from jax.sharding import PartitionSpec as P

W = 384
BLK = 128
SUPER = 3
precise = lax.Precision.HIGHEST


def product(left, right):
    return jnp.dot(left, right, precision=precise, preferred_element_type=jnp.float32)


def inner_product(left, right):
    return lax.dot_general(
        left, right, (((0,), (0,)), ((), ())), precision=precise, preferred_element_type=jnp.float32
    )


def outer_product(left, right):
    return lax.dot_general(
        left, right, (((1,), (1,)), ((), ())), precision=precise, preferred_element_type=jnp.float32
    )


def tile_pattern(tile_mask, first_block, blocks):
    window = lax.dynamic_slice_in_dim(tile_mask, first_block, blocks, 1).astype(jnp.float32)
    window = jnp.transpose(window, (1, 0, 2))
    widened = jnp.broadcast_to(window[:, None, :, :, None], (blocks, BLK, SUPER, W // BLK, BLK))
    return widened.reshape(blocks * BLK, SUPER, W)


def row_term(anc_inverse, lower_cols):
    return product(anc_inverse, lower_cols)


def col_term(anc_inverse, upper_rows):
    return inner_product(anc_inverse, upper_rows)


def per_device(anc_inverse, lower_anc, upper_anc, lower_edge, upper_edge, diag_inverse, tile_mask):
    rows_here, cols_here = anc_inverse.shape
    slab_rows = rows_here // lax.axis_size("col")
    row_index = lax.axis_index("row")
    col_index = lax.axis_index("col")
    col_pattern = tile_pattern(tile_mask, col_index * (cols_here // BLK), cols_here // BLK)
    row_pattern = tile_pattern(tile_mask, row_index * (rows_here // BLK), rows_here // BLK)
    lower_list = []
    upper_list = []
    cols_list = []
    rows_list = []
    lower_full = lax.all_gather(lower_anc, "row", axis=2, tiled=True) * col_pattern
    upper_full = lax.all_gather(upper_anc, "col", axis=2, tiled=True) * row_pattern
    cols_all = lax.psum_scatter(
        row_term(anc_inverse, lower_full.reshape(cols_here, SUPER * W)),
        "col",
        scatter_dimension=0,
        tiled=True,
    )
    rows_all = lax.psum_scatter(
        col_term(anc_inverse, upper_full.reshape(rows_here, SUPER * W)),
        "row",
        scatter_dimension=0,
        tiled=True,
    )
    cols_all = cols_all.reshape(slab_rows, SUPER, W)
    rows_all = rows_all.reshape(slab_rows, SUPER, W)
    for node_index in range(SUPER):
        lower_list.append(lower_full[:, node_index, :])
        upper_list.append(upper_full[:, node_index, :])
        cols_list.append(cols_all[:, node_index, :])
        rows_list.append(rows_all[:, node_index, :])
    x_list = []
    y_list = []
    corner_list = []
    cross_cols = []
    cross_rows = []
    for node_index in range(SUPER):
        lower_cur = lower_list[node_index]
        upper_cur = upper_list[node_index]
        inv_cols = -cols_list[node_index]
        inv_rows = -rows_list[node_index]
        upper_mine = lax.dynamic_slice_in_dim(upper_cur, col_index * slab_rows, slab_rows, 0)
        if node_index > 0:
            lower_side = lower_edge[node_index - 1]
            upper_side = upper_edge[node_index - 1]
            lower_mine = lax.dynamic_slice_in_dim(lower_cur, row_index * slab_rows, slab_rows, 0)
            rows_lower = inner_product(prev_rows, lower_mine)
            upper_cols = inner_product(upper_mine, prev_cols)
        if node_index > 0:
            rows_lower, upper_cols = lax.psum((rows_lower, upper_cols), ("row", "col"))
        if node_index > 0:
            cross_col = -(rows_lower + product(prev_corner, lower_side))
            cross_row = -(upper_cols + product(upper_side, prev_corner))
            inv_cols = inv_cols - product(prev_cols, lower_side)
            inv_rows = inv_rows - outer_product(prev_rows, upper_side)
            cross_cols.append(cross_col)
            cross_rows.append(cross_row)
        inv_corner = diag_inverse[node_index] - lax.psum(
            inner_product(upper_mine, inv_cols), ("row", "col")
        )
        if node_index > 0:
            inv_corner = inv_corner - product(upper_side, cross_col)
        x_list.append(inv_cols)
        y_list.append(inv_rows)
        corner_list.append(inv_corner)
        prev_cols = inv_cols
        prev_rows = inv_rows
        prev_corner = inv_corner
    x_blocks = jnp.stack(x_list, axis=1)
    y_blocks = jnp.stack(y_list, axis=1)[None, None]
    tile_rows = W // lax.axis_size("row")
    tile_cols = W // lax.axis_size("col")
    corners = jnp.stack(corner_list)
    corners = lax.dynamic_slice_in_dim(corners, row_index * tile_rows, tile_rows, 1)
    z_blocks = lax.dynamic_slice_in_dim(corners, col_index * tile_cols, tile_cols, 2)
    crossed = jnp.stack([jnp.stack(cross_cols), jnp.stack(cross_rows)])
    crossed = lax.dynamic_slice_in_dim(crossed, row_index * tile_rows, tile_rows, 2)
    cross_blocks = lax.dynamic_slice_in_dim(crossed, col_index * tile_cols, tile_cols, 3)
    return (x_blocks, y_blocks, z_blocks, cross_blocks)


def solution(mesh):
    return jax.shard_map(
        per_device,
        mesh=mesh,
        in_specs=(
            P("row", "col"),
            P("col", None, "row"),
            P("row", None, "col"),
            P(),
            P(),
            P(),
            P(),
        ),
        out_specs=(
            P(("row", "col"), None, None),
            P("col", "row", None, None, None),
            P(None, "row", "col"),
            P(None, None, "row", "col"),
        ),
        check_vma=False,
    )
```

profile of v0, /device:TPU:0, one launch (start us, length us, event | category | flops | bytes accessed | tf_op | source)
XLA Modules:
  0.0 565.6 jit_solution(17613502817447202190)
XLA Ops:
  8.9 4.2 broadcast_in_dim.6
  13.1 10.5 %reshape.42 = f32[1280,3,384]{2,0,1:T(8,128)} reshape(f32[10,128,3,3,128]{4,3,1,0,2:T(4,128)} %broadcast_in_dim.6) | data formatting | bytes 11796480 | tf_op jit(solution)/shard_map/reshape | solution.py:32
  23.6 55.8 %all-gather.3.cloned.1.call-done = f32[1280,3,384]{0,2,1:T(8,128)} async-done(((f32[1280,3,96]{0,2,1:T(8,128)}), f32[1280,3,384]{0,2,1:T(8,128)}) %all-gather.3.cloned.1.call-update) | async-done | bytes 5898256 | tf_op jit(solution)/shard_map/all_gather | solution.py:54
  79.3 7.7 %copy.70 = f32[1280,3,384]{2,0,1:T(8,128)} copy(f32[1280,3,384]{0,2,1:T(8,128)} %all-gather.3.cloned.1.call-done) | data formatting | bytes 11796480 | tf_op jit(solution)/shard_map/all_gather | solution.py:54
  87.0 9.3 %mul.30 = f32[1280,3,384]{2,0,1:T(8,128)} multiply(f32[1280,3,384]{2,0,1:T(8,128)} %copy.70, f32[1280,3,384]{2,0,1:T(8,128)} %reshape.42) | non-fusion elementwise | flops 1474560 | bytes 17694720 | tf_op jit(solution)/shard_map/mul | solution.py:54
  96.3 7.8 %copy.71 = f32[1280,3,384]{0,2,1:T(8,128)} copy(f32[1280,3,384]{2,0,1:T(8,128)} %mul.30) | data formatting | bytes 11796480 | tf_op jit(solution)/shard_map/mul | solution.py:54
  104.0 52.7 %convolution_bitcast_fusion = f32[2560,1152]{0,1:T(8,128)} fusion(f32[1280,1152]{0,1:T(8,128)} %bitcast.163, f32[2560,1280]{1,0:T(8,128)} %param.7), kind=kOutput, calls=%fused_computation | convolution fusion | flops 45298483200 | bytes 30801920 | tf_op jit(solution)/shard_map/dot_general | solution.py:13
  156.8 13.6 %copy.92 = f32[2560,1152]{1,0:T(8,128)} copy(f32[2560,1152]{0,1:T(8,128)} %convolution_bitcast_fusion) | data formatting | bytes 23592960
  171.1 6.0 %broadcast_in_dim.7 = f32[20,128,3,3,128]{1,0,4,3,2:T(8,128)} broadcast(f32[20,3,3]{0,2,1:T(4,128)S(1)} %convert_bitcast_fusion), dimensions={0,2,3} | broadcast | bytes 11797200 | tf_op jit(solution)/shard_map/broadcast_in_dim | solution.py:31
  177.1 13.7 %reshape.45 = f32[2560,3,384]{0,2,1:T(8,128)} reshape(f32[20,128,3,3,128]{1,0,4,3,2:T(8,128)} %broadcast_in_dim.7) | data formatting | bytes 23592960 | tf_op jit(solution)/shard_map/reshape | solution.py:32
  191.2 9.7 %mul.32 = f32[2560,3,384]{0,2,1:T(8,128)S(1)} multiply(f32[2560,3,384]{0,2,1:T(8,128)} %all-gather.5.cloned.1.call-done, f32[2560,3,384]{0,2,1:T(8,128)} %reshape.45) | non-fusion elementwise | flops 2949120 | bytes 35389440 | tf_op jit(solution)/shard_map/mul | solution.py:55
  200.9 4.3 copy-done
  205.3 50.1 %convolution_bitcast_fusion.1 = f32[1280,1152]{0,1:T(8,128)} fusion(f32[2560,1152]{0,1:T(8,128)S(1)} %bitcast.157, f32[2560,1280]{1,0:T(8,128)} %param.7), kind=kOutput, calls=%fused_computation.1 | convolution fusion | flops 45298483200 | bytes 30801920 | tf_op jit(solution)/shard_map/dot_general | solution.py:17
  255.4 7.7 %copy.94 = f32[1280,1152]{1,0:T(8,128)} copy(f32[1280,1152]{0,1:T(8,128)} %convolution_bitcast_fusion.1) | data formatting | bytes 11796480
  263.3 4.3 fusion.75
  267.6 9.3 %fusion.74 = (f32[2560,1,384]{0,2,1:T(8,128)}, f32[2560,1,384]{0,2,1:T(8,128)}, f32[2560,1,384]{0,2,1:T(8,128)}) fusion(f32[2560,3,384]{0,2,1:T(8,128)} %copy-done), kind=kLoop, calls=%fused_computation.100 | loop fusion | bytes 23592960 | tf_op jit(solution)/shard_map/slice | solution.py:72
  276.9 36.6 %reduce-scatter.7.cloned.1.call-done = f32[320,1152]{1,0:T(8,128)} async-done(((f32[2560,1152]{1,0:T(8,128)}), f32[320,1152]{1,0:T(8,128)}) %reduce-scatter.7.cloned.1.call-update) | async-done | bytes 1474576
  313.5 2.1 copy.93
  319.1 3.3 fusion.16
  323.5 3.3 fusion.18
  326.7 3.3 fusion.12
  331.9 3.2 fusion.14
  335.1 46.5 %reduce-scatter.9.cloned.1.call-done = f32[320,1152]{1,0:T(8,128)} async-done(((f32[1280,1152]{1,0:T(8,128)}), f32[320,1152]{1,0:T(8,128)}) %reduce-scatter.9.cloned.1.call-update) | async-done | bytes 1474576
  381.6 2.3 copy.95
  386.6 2.1 copy.100
  388.7 3.3 fusion.20
  393.1 3.2 fusion.49
  396.3 3.2 fusion.47
  402.5 2.2 pad_maximum_fusion
  407.0 137.7 %all-reduce.3.cloned.1.call-done = (f32[384,384]{1,0:T(8,128)}, f32[384,384]{1,0:T(8,128)}, f32[384,384]{1,0:T(8,128)}, f32[384,384]{1,0:T(8,128)}, f32[384,384]...) async-done(((f32[384,384]{1,0:T(8,128)}, f32[384,384]{1,0:T(8,128)}, f32[384,384]{1,0:T(8,128)}, f32[384,384]{1,0:T(8,128)}, f32[384,384]{1,0:T(8,128)}, ...) | async-done | bytes 4128784 | tf_op jit(solution)/shard_map/psum | solution.py:101
  546.3 2.5 fusion.7
  555.4 2.5 fusion.9
  (71 shorter events, 27.2 us)
Async XLA Ops:
  7.2 1.5 copy-start.16
  7.2 72.2 %all-gather.3.cloned.1.call-start = ((), (), s32[]{:S(2)}) async-start(), calls=%async_computation.2 | async-start | bytes 7372800 | tf_op jit(solution)/shard_map/all_gather | solution.py:54
  7.9 183.3 %all-gather.5.cloned.1.call-start = ((), (), s32[]{:S(2)}) async-start(), calls=%async_computation.3 | async-start | bytes 13271040 | tf_op jit(solution)/shard_map/all_gather | solution.py:55
  8.7 304.8 %reduce-scatter.7.cloned.1.call-start = ((), (), s32[]{:S(2)}) async-start(), calls=%async_computation.4 | async-start | bytes 13271040
  170.4 211.2 %reduce-scatter.9.cloned.1.call-start = ((), (), s32[]{:S(2)}) async-start(), calls=%async_computation.5 | async-start | bytes 7372800
  200.9 4.3 copy-start
  263.1 281.6 %all-reduce.3.cloned.1.call-start = ((), (), s32[]{:S(2)}) async-start(), calls=%async_computation.6 | async-start | bytes 8257536 | tf_op jit(solution)/shard_map/psum | solution.py:101
  317.8 4.5 copy-start.4
  319.1 3.3 copy-start.9
  331.1 0.8 copy-start.6
  385.2 6.8 %copy-start.1 = (f32[2,384,384]{2,1,0:T(8,128)S(1)}, f32[2,384,384]{2,1,0:T(8,128)}, u32[]{:S(2)}) copy-start(f32[2,384,384]{2,1,0:T(8,128)} %param.11) | copy-start | bytes 3538948
  388.7 3.3 copy-start.10
  400.4 2.1 copy-start.7
  404.7 1.1 copy-start.8
  544.7 1.5 copy-start.2
  544.7 1.6 copy-start.15
  544.7 4.2 copy-start.14
  546.1 2.7 copy-start.3
  546.1 2.7 copy-start.5
  548.8 1.3 copy-start.13
  550.1 1.3 copy-start.12
  551.5 1.6 copy-start.11
Sparse Core Ops, SparseCore 0:
  9.8 69.4 all-gather.2
  81.0 110.1 all-gather.4
  193.5 119.9 reduce-scatter.6
  316.4 65.2 reduce-scatter.8
  399.6 144.9 all-reduce.2
where the time goes:
time: 574 us; the launch traced here: 566 us
  waiting for transfers between devices  278 us (48%)
  matrix products  140 us (24%)
  local copies, waits for them, and re-layouts  105 us (18%)
  other arithmetic  26.1 us (5%)
  between operations  14.4 us (3%)
    psum x1, waiting for transfers between devices, per_device(): lax.psum(inner_product(upper_mine, inv_cols), ('row', 'col'))  138 us
    unnamed x7, waiting for transfers between devices  84.6 us
    dot_general x8, matrix products, inner_product(): lax.dot_general(left, right, (((0,), (0,)), ((), ())), precision=precise,...  72.9 us
    dot_general x9, matrix products, product(): jnp.dot(left, right, precision=precise, preferred_element_type=jnp.float32)  65.3 us
    all_gather x1, waiting for transfers between devices, per_device(): lax.all_gather(lower_anc, 'row', axis=2, tiled=True) * col_pattern  55.8 us
    unnamed x46, local copies, waits for them, and re-layouts  39.8 us
    reshape x2, local copies, waits for them, and re-layouts, tile_pattern(): return widened.reshape(blocks * BLK, SUPER, W)  24.2 us
  transfers between devices with their start and end apart: 5, of which 5 were waited for; matrix products, arithmetic and copies ran while one was open for 42% of the time, Pallas kernels for 0%

commit v1 on v0

--- a/solution.py
+++ b/solution.py
@@ -7,6 +7,12 @@
 BLK = 128
 SUPER = 3
 precise = lax.Precision.HIGHEST
+
+
+def stack_and_merge(shard, axis, dim):
+    blocks = lax.all_gather(shard, axis, axis=0, tiled=False)
+    whole = jnp.concatenate(blocks, axis=dim)
+    return whole
 
 
 def product(left, right):
@@ -51,7 +57,7 @@
     upper_list = []
     cols_list = []
     rows_list = []
-    lower_full = lax.all_gather(lower_anc, "row", axis=2, tiled=True) * col_pattern
+    lower_full = stack_and_merge(lower_anc, "row", 2) * col_pattern
     upper_full = lax.all_gather(upper_anc, "col", axis=2, tiled=True) * row_pattern
     cols_all = lax.psum_scatter(
         row_term(anc_inverse, lower_full.reshape(cols_here, SUPER * W)),

time: 574 us -> 572 us (level)
  local copies, waits for them, and re-layouts: 105 us -> 114 us
  waiting for transfers between devices: 278 us -> 270 us
  matrix products: 140 us -> 147 us
    unnamed x7, waiting for transfers between devices: 84.6 us -> 59.4 us
    all_gather x1, waiting for transfers between devices: 55.8 us -> 70.5 us  [stack_and_merge(): blocks = lax.all_gather(shard, axis, axis=0, tiled=False)]
    mul x1 -> x0, local copies, waits for them, and re-layouts: 7.76 us -> none  [per_device(): lax.all_gather(lower_anc, 'row', axis=2, tiled=True) * col_pattern]
    reshape x2 -> x3, local copies, waits for them, and re-layouts: 24.2 us -> 31.9 us  [tile_pattern(): return widened.reshape(blocks * BLK, SUPER, W)]
    broadcast_in_dim x2 -> x3, local copies, waits for them, and re-layouts: 10.2 us -> 14.8 us  [tile_pattern(): jnp.broadcast_to(window[:, None, :, :, None], (blocks, BLK, SUPER, W // B...]
    unnamed x46 -> x48, local copies, waits for them, and re-layouts: 39.8 us -> 40.5 us
  transfers between devices with their start and end apart: 5 -> 5, of which waited for: 5 -> 5; matrix products, arithmetic and copies ran while one was open for 42% -> 43% of each run, Pallas kernels for 0% -> 0%
where the time goes in v1:
time: 572 us; the launch traced here: 568 us
  waiting for transfers between devices  270 us (47%)
  matrix products  147 us (26%)
  local copies, waits for them, and re-layouts  114 us (20%)
  other arithmetic  22.1 us (4%)
  between operations  14.4 us (3%)
    psum x1, waiting for transfers between devices, per_device(): lax.psum(inner_product(upper_mine, inv_cols), ('row', 'col'))  137 us
    dot_general x8, matrix products, inner_product(): lax.dot_general(left, right, (((0,), (0,)), ((), ())), precision=precise,...  74.8 us
    all_gather x1, waiting for transfers between devices, stack_and_merge(): blocks = lax.all_gather(shard, axis, axis=0, tiled=False)  70.5 us
    dot_general x9, matrix products, product(): jnp.dot(left, right, precision=precise, preferred_element_type=jnp.float32)  69.9 us
    unnamed x7, waiting for transfers between devices  59.4 us
    unnamed x48, local copies, waits for them, and re-layouts  40.5 us
    reshape x3, local copies, waits for them, and re-layouts, tile_pattern(): return widened.reshape(blocks * BLK, SUPER, W)  31.9 us
    broadcast_in_dim x3, local copies, waits for them, and re-layouts, tile_pattern(): jnp.broadcast_to(window[:, None, :, :, None], (blocks, BLK, SUPER, W // B...  14.8 us
  transfers between devices with their start and end apart: 5, of which 5 were waited for; matrix products, arithmetic and copies ran while one was open for 43% of the time, Pallas kernels for 0%

profile of v1, /device:TPU:0, one launch (start us, length us, event | category | flops | bytes accessed | tf_op | source)
XLA Modules:
  0.0 567.6 jit_solution(2790890702815255923)
XLA Ops:
  8.8 70.5 %all-gather.6.cloned.1.call-done = f32[5120,3,96]{0,2,1:T(8,128)} async-done(((f32[1280,3,96]{0,2,1:T(8,128)}), f32[5120,3,96]{0,2,1:T(8,128)}) %all-gather.6.cloned.1.call-update) | async-done | bytes 5898256 | tf_op jit(solution)/shard_map/all_gather | solution.py:13
  79.3 8.2 %reshape.61 = f32[4,1280,3,96]{1,0,3,2:T(4,128)} reshape(f32[5120,3,96]{0,2,1:T(8,128)} %all-gather.6.cloned.1.call-done) | data formatting | bytes 11796480 | tf_op jit(solution)/shard_map/all_gather | solution.py:13
  87.6 4.4 copy.78
  92.0 4.6 broadcast_in_dim.6.clone
  97.4 57.3 %convolution_bitcast_fusion = f32[2560,1152]{0,1:T(8,128)} fusion(f32[2560,1280]{1,0:T(8,128)} %param.7, f32[1280,1152]{0,1:T(8,128)S(1)} %bitcast.173, f32[144,8,10,128]{3,2,1,0:T(8,128)} %bitcast.176), kind=kOutput, calls=%fused_computation | convolution fusion | flops 45299957760 | bytes 36700160 | tf_op jit(solution)/shard_map/dot_general | solution.py:19
  154.7 13.6 %copy.105 = f32[2560,1152]{1,0:T(8,128)} copy(f32[2560,1152]{0,1:T(8,128)} %convolution_bitcast_fusion) | data formatting | bytes 23592960
  168.4 6.0 %broadcast_in_dim.7 = f32[20,128,3,3,128]{1,0,4,3,2:T(8,128)} broadcast(f32[20,3,3]{0,2,1:T(4,128)S(1)} %convert_bitcast_fusion), dimensions={0,2,3} | broadcast | bytes 11797200 | tf_op jit(solution)/shard_map/broadcast_in_dim | solution.py:37
  174.4 13.7 %reshape.56 = f32[2560,3,384]{0,2,1:T(8,128)} reshape(f32[20,128,3,3,128]{1,0,4,3,2:T(8,128)} %broadcast_in_dim.7) | data formatting | bytes 23592960 | tf_op jit(solution)/shard_map/reshape | solution.py:38
  188.1 3.0 all-gather.4.cloned.1.call-done
  191.2 9.7 %mul.35 = f32[2560,3,384]{0,2,1:T(8,128)S(1)} multiply(f32[2560,3,384]{0,2,1:T(8,128)} %all-gather.4.cloned.1.call-done, f32[2560,3,384]{0,2,1:T(8,128)} %reshape.56) | non-fusion elementwise | flops 2949120 | bytes 35389440 | tf_op jit(solution)/shard_map/mul | solution.py:61
  200.9 4.3 copy-done
  205.3 50.0 %convolution_bitcast_fusion.1 = f32[1280,1152]{0,1:T(8,128)} fusion(f32[2560,1152]{0,1:T(8,128)S(1)} %bitcast.172, f32[2560,1280]{1,0:T(8,128)} %param.7), kind=kOutput, calls=%fused_computation.1 | convolution fusion | flops 45298483200 | bytes 30801920 | tf_op jit(solution)/shard_map/dot_general | solution.py:23
  255.3 7.7 %copy.107 = f32[1280,1152]{1,0:T(8,128)} copy(f32[1280,1152]{0,1:T(8,128)} %convolution_bitcast_fusion.1) | data formatting | bytes 11796480
  263.1 4.2 broadcast_in_dim.6
  267.3 10.5 %reshape.60 = f32[1280,3,384]{2,0,1:T(8,128)} reshape(f32[10,128,3,3,128]{4,3,1,0,2:T(4,128)} %broadcast_in_dim.6) | data formatting | bytes 11796480 | tf_op jit(solution)/shard_map/reshape | solution.py:38
  277.8 7.7 %copy.89 = f32[1280,3,384]{0,2,1:T(8,128)} copy(f32[1280,3,384]{2,0,1:T(8,128)} %reshape.60) | data formatting | bytes 11796480 | tf_op jit(solution)/shard_map/reshape | solution.py:38
  285.5 5.2 bitcast_multiply_fusion.2
  292.9 9.2 %fusion.75 = (f32[2560,1,384]{0,2,1:T(8,128)}, f32[2560,1,384]{0,2,1:T(8,128)}, f32[2560,1,384]{0,2,1:T(8,128)}) fusion(f32[2560,3,384]{0,2,1:T(8,128)} %copy-done), kind=kLoop, calls=%fused_computation.103 | loop fusion | bytes 23592960 | tf_op jit(solution)/shard_map/slice | solution.py:78
  302.1 11.4 %reduce-scatter.7.cloned.1.call-done = f32[320,1152]{1,0:T(8,128)} async-done(((f32[2560,1152]{1,0:T(8,128)}), f32[320,1152]{1,0:T(8,128)}) %reduce-scatter.7.cloned.1.call-update) | async-done | bytes 1474576
  319.1 3.3 fusion.21
  323.5 3.2 fusion.23
  326.7 3.3 fusion.15
  331.9 3.2 fusion.17
  335.1 46.5 %reduce-scatter.9.cloned.1.call-done = f32[320,1152]{1,0:T(8,128)} async-done(((f32[1280,1152]{1,0:T(8,128)}), f32[320,1152]{1,0:T(8,128)}) %reduce-scatter.9.cloned.1.call-update) | async-done | bytes 1474576
  381.6 2.3 copy.108
  388.7 3.3 fusion.25
  393.1 4.2 fusion.19
  397.3 4.2 fusion.13
  404.5 2.3 pad_maximum_fusion
  409.1 137.5 %all-reduce.3.cloned.1.call-done = (f32[384,384]{1,0:T(8,128)}, f32[384,384]{1,0:T(8,128)}, f32[384,384]{1,0:T(8,128)}, f32[384,384]{1,0:T(8,128)}, f32[384,384]...) async-done(((f32[384,384]{1,0:T(8,128)}, f32[384,384]{1,0:T(8,128)}, f32[384,384]{1,0:T(8,128)}, f32[384,384]{1,0:T(8,128)}, f32[384,384]{1,0:T(8,128)}, ...) | async-done | bytes 4128784 | tf_op jit(solution)/shard_map/psum | solution.py:107
  548.2 2.6 fusion.8
  557.4 2.5 fusion.10
  (75 shorter events, 33.3 us)
Async XLA Ops:
  7.2 1.5 copy-start.17
  7.2 72.2 %all-gather.6.cloned.1.call-start = ((), (), s32[]{:S(2)}) async-start(), calls=%async_computation.3 | async-start | bytes 7372800 | tf_op jit(solution)/shard_map/all_gather | solution.py:13
  7.9 183.3 %all-gather.4.cloned.1.call-start = ((), (), s32[]{:S(2)}) async-start(), calls=%async_computation.2 | async-start | bytes 13271040 | tf_op jit(solution)/shard_map/all_gather | solution.py:61
  8.7 304.8 %reduce-scatter.7.cloned.1.call-start = ((), (), s32[]{:S(2)}) async-start(), calls=%async_computation.4 | async-start | bytes 13271040
  92.0 5.4 copy-start.1
  168.2 213.4 %reduce-scatter.9.cloned.1.call-start = ((), (), s32[]{:S(2)}) async-start(), calls=%async_computation.5 | async-start | bytes 7372800
  200.9 4.3 copy-start
  263.0 283.6 %all-reduce.3.cloned.1.call-start = ((), (), s32[]{:S(2)}) async-start(), calls=%async_computation.6 | async-start | bytes 8257536 | tf_op jit(solution)/shard_map/psum | solution.py:107
  317.8 4.5 copy-start.5
  319.0 3.3 copy-start.10
  331.1 0.8 copy-start.7
  385.2 6.8 %copy-start.2 = (f32[2,384,384]{2,1,0:T(8,128)S(1)}, f32[2,384,384]{2,1,0:T(8,128)}, u32[]{:S(2)}) copy-start(f32[2,384,384]{2,1,0:T(8,128)} %param.11) | copy-start | bytes 3538948
  388.7 3.3 copy-start.11
  402.4 2.1 copy-start.8
  404.5 3.4 copy-start.9
  546.6 1.5 copy-start.3
  546.6 1.6 copy-start.16
  546.6 4.2 copy-start.4
  546.6 4.2 copy-start.6
  546.6 4.2 copy-start.15
  550.8 1.3 copy-start.14
  552.1 1.6 copy-start.13
  552.1 2.9 copy-start.12
Sparse Core Ops, SparseCore 0:
  9.8 69.4 all-gather.5
  80.9 110.1 all-gather.3
  193.5 119.9 reduce-scatter.6
  316.4 65.2 reduce-scatter.8
  401.7 144.9 all-reduce.2
